TPU v7x, 128 devices: a whole 4x4x4 slice. The times are simulated.
128 devices in a mesh: outer: 8 (over x, z_lo), inner: 16 (over z_hi, y, core).
Axes of the slice: x: 4, y: 4, z: 4 (z_hi: 2, z_lo: 2; z = z_hi * 2 + z_lo), core: 2. Of those that a mesh axis runs over, the one named last changes fastest.
Arguments:
- gate_in: bfloat16 [16384, 4096], P(('outer', 'inner')), may hold values from -6 to 6
- value_in: bfloat16 [16384, 4096], P(('outer', 'inner')), may hold values from -6 to 6
- gate_out: bfloat16 [16384, 4096], P(('outer', 'inner')), may hold values from -6 to 6
- filters: bfloat16 [16384, 4096], P(('outer', 'inner')), may hold values from -1.04 to 1.04
- skip_bias: float32 [4096], replicated, may hold values from 0.5 to 1.5
Outputs:
- mixer_out: bfloat16 [16384, 4096], P(('outer', 'inner'))
All inputs are finite; a program needn't handle non-finite values.
Results may differ from a plain program's by a relative error of at most 0.009.
Values may be sent and summed in bfloat16 or wider, within the bound.
A program may use at most 128 MiB of HBM per device.

v0:
```python
import math

import jax
import jax.numpy as jnp
from jax import lax
from jax.sharding import PartitionSpec as P

highest = lax.Precision.HIGHEST


def phasor(counts, period):
    angles = (counts % period).astype(jnp.float32) * (2.0 * math.pi / period)
    return (jnp.cos(angles), jnp.sin(angles))


def rotate(real_part, imag_part, cosine, sine_part, orient):
    return (
        real_part * cosine - orient * imag_part * sine_part,
        imag_part * cosine + orient * real_part * sine_part,
    )


def shards(gate_in, value_in, gate_out, filters, skip_bias):
    n_outer = lax.axis_size("outer")
    n_inner = lax.axis_size("inner")
    groups = n_outer * n_inner
    block_rows, channels = gate_in.shape
    slab_rows = block_rows // groups
    seq_length = block_rows * groups
    modulated = (gate_in.astype(jnp.float32) * value_in.astype(jnp.float32)).astype(jnp.bfloat16)
    token_places = jnp.arange(groups, dtype=jnp.int32)
    frequency = jnp.arange(groups, dtype=jnp.int32)
    branch = jnp.arange(2, dtype=jnp.int32)
    within = jnp.arange(slab_rows, dtype=jnp.int32)
    own_freq = lax.axis_index("outer") * n_inner + lax.axis_index("inner")
    stacked = jnp.stack([modulated, filters])[None]
    spread = lax.all_to_all(stacked, ("outer", "inner"), split_axis=2, concat_axis=0, tiled=True)
    counts = token_places[None, None, :] * (2 * frequency[None, :, None] + branch[:, None, None])
    cosine, sine_part = phasor(counts, 2 * groups)
    kernel = jnp.stack([cosine, -sine_part], axis=1)
    cross_rows = jnp.einsum(
        "rukp,pamc->kruamc", kernel, spread.astype(jnp.float32), precision=highest
    )
    cross_rows = cross_rows.reshape(groups, 1, 8, slab_rows, channels)
    received = lax.all_to_all(
        cross_rows, ("outer", "inner"), split_axis=0, concat_axis=1, tiled=True
    )
    spectra = received.reshape(groups, 2, 2, 2, slab_rows, channels)
    offsets = token_places[:, None] * slab_rows + within[None, :]
    counts = offsets[:, None, :] * (2 * own_freq + branch)[None, :, None]
    cosine, sine_part = phasor(counts, 2 * seq_length)
    real_part, imag_part = rotate(
        spectra[:, :, 0],
        spectra[:, :, 1],
        cosine[:, :, None, :, None],
        sine_part[:, :, None, :, None],
        -1.0,
    )
    cos_rows, sin_rows = phasor(frequency[:, None] * token_places[None, :], groups)

    def over_rows(matrix, values):
        return jnp.einsum("kp,prajc->krajc", matrix, values, precision=highest)

    first_real = over_rows(cos_rows, real_part) + over_rows(sin_rows, imag_part)
    first_imag = over_rows(cos_rows, imag_part) - over_rows(sin_rows, real_part)
    cosine, sine_part = phasor(frequency[:, None] * within[None, :], block_rows)
    turn_real, turn_imag = rotate(
        first_real,
        first_imag,
        cosine[:, None, None, :, None],
        sine_part[:, None, None, :, None],
        -1.0,
    )
    cos_slab, sin_slab = phasor(within[:, None] * within[None, :], slab_rows)

    def over_slab(matrix, values):
        return jnp.einsum("qj,krajc->kraqc", matrix, values, precision=highest)

    spec_real = over_slab(cos_slab, turn_real) + over_slab(sin_slab, turn_imag)
    spec_imag = over_slab(cos_slab, turn_imag) - over_slab(sin_slab, turn_real)
    signal_real, signal_imag = (spec_real[:, :, 0], spec_imag[:, :, 0])
    filter_real, filter_imag = (spec_real[:, :, 1], spec_imag[:, :, 1])
    product_real = signal_real * filter_real - signal_imag * filter_imag
    product_imag = signal_real * filter_imag + signal_imag * filter_real

    def back_slab(matrix, values):
        return jnp.einsum("jq,krqc->krjc", matrix, values, precision=highest)

    inner_real = back_slab(cos_slab, product_real) - back_slab(sin_slab, product_imag)
    inner_imag = back_slab(cos_slab, product_imag) + back_slab(sin_slab, product_real)
    cosine, sine_part = phasor(frequency[:, None] * within[None, :], block_rows)
    inner_real, inner_imag = rotate(
        inner_real, inner_imag, cosine[:, None, :, None], sine_part[:, None, :, None], 1.0
    )
    cos_back, sin_back = phasor(frequency[:, None] * frequency[None, :], groups)

    def back_rows(matrix, values):
        return jnp.einsum("bk,krjc->rbjc", matrix, values, precision=highest)

    outer_real = back_rows(cos_back, inner_real) - back_rows(sin_back, inner_imag)
    outer_imag = back_rows(cos_back, inner_imag) + back_rows(sin_back, inner_real)
    spots = frequency[:, None] * slab_rows + within[None, :]
    counts = spots[None, :, :] * (2 * own_freq + branch)[:, None, None]
    cosine, sine_part = phasor(counts, 2 * seq_length)
    outer_real, outer_imag = rotate(
        outer_real, outer_imag, cosine[..., None], sine_part[..., None], 1.0
    )
    leaving = jnp.stack([outer_real, outer_imag], axis=1).reshape(1, 4, block_rows, channels)
    arrived = lax.all_to_all(leaving, ("outer", "inner"), split_axis=2, concat_axis=0, tiled=True)
    counts = frequency[:, None, None] * (2 * token_places[None, :, None] + branch[None, None, :])
    cosine, sine_part = phasor(counts, 2 * groups)
    kernel = jnp.stack([cosine, -sine_part], axis=-1).reshape(groups, 4 * groups)
    values = arrived.reshape(4 * groups, slab_rows * channels)
    partial_rows = jnp.dot(kernel, values, precision=highest) * (1.0 / (2.0 * seq_length))
    partial_rows = partial_rows.reshape(groups, 1, slab_rows, channels)
    assembled = lax.all_to_all(
        partial_rows, ("outer", "inner"), split_axis=0, concat_axis=1, tiled=True
    )
    convolved = assembled.reshape(block_rows, channels)
    result = gate_out.astype(jnp.float32) * (
        convolved + skip_bias[None, :] * modulated.astype(jnp.float32)
    )
    return result.astype(jnp.bfloat16)


def solution(mesh):
    placed = (
        P(("outer", "inner"), None),
        P(("outer", "inner"), None),
        P(("outer", "inner"), None),
        P(("outer", "inner"), None),
        P(),
    )
    return jax.shard_map(
        shards, mesh=mesh, in_specs=placed, out_specs=P(("outer", "inner"), None), check_vma=False
    )
```

profile of v0, /device:TPU:0, one launch (start us, length us, event | category | flops | bytes accessed | tf_op | source)
XLA Modules:
  0.0 663.5 jit_solution(11209583515993808884)
XLA Ops:
  3.2 3.5 copy.100
  6.7 11.7 %all-to-all-start = ((bf16[1,2,128,4096]{3,1,0,2:T(2,128)(2,1)}), bf16[1,2,128,4096]{3,1,0,2:T(2,128)(2,1)}, u32[]{:S(2)}, u32[]{:S(2)}) async-start(bf16[1,2,128,4096]{3,1,0,2:T(2,128)(2,1)} %copy.100), calls=%async_computation | async-start | bytes 4194304 | tf_op jit(solution)/shard_map/all_to_all | solution.py:37
  19.6 28.6 %all-to-all-done = bf16[1,2,128,4096]{3,1,0,2:T(2,128)(2,1)} async-done(((bf16[1,2,128,4096]{3,1,0,2:T(2,128)(2,1)}), bf16[1,2,128,4096]{3,1,0,2:T(2,128)(2,1)}, u32[]{:S(2)}, u32[]{:S(2)}) %all-to-all-start) | async-done | bytes 2097184 | tf_op jit(solution)/shard_map/all_to_all | solution.py:37
  48.2 4.9 copy.101
  53.1 9.5 %convolution_bitcast_fusion = f32[128,2,2,2,1,4096]{0,5,2,1,3,4:T(8,128)} fusion(bf16[1,2,128,4096]{2,3,1,0:T(8,128)(2,1)S(1)} %copy.101, f32[2,1,128,128]{3,2,1,0:T(8,128)S(1)} %get-tuple-element.15, f32[2,1,128,128]{3,2,1,0:T(8,128)S(1)} %get-tuple-element.14), kind=kOutput, calls=%fused_computation | convolution fusion | flops 6442516480 | bytes 19136512 | tf_op jit(solution)/shard_map/rukp,pamc->kruamc/dot_general | solution.py:41
  62.6 17.5 %copy.102 = f32[128,2,2,2,1,4096]{5,0,3,2,1,4:T(8,128)} copy(f32[128,2,2,2,1,4096]{0,5,2,1,3,4:T(8,128)} %convolution_bitcast_fusion) | data formatting | bytes 33554432 | tf_op jit(solution)/shard_map/rukp,pamc->kruamc/transpose | solution.py:41
  80.1 17.7 %copy.103 = f32[128,1,8,1,4096]{4,2,3,1,0:T(8,128)} copy(f32[128,1,8,1,4096]{4,0,2,3,1:T(8,128)} %bitcast.136) | data formatting | bytes 33554432 | tf_op jit(solution)/shard_map/reshape | solution.py:44
  97.8 6.2 all-to-all-start.1
  104.3 230.2 %all-to-all-done.1 = f32[128,1,8,1,4096]{4,2,3,1,0:T(8,128)} async-done(((f32[128,1,8,1,4096]{4,2,3,1,0:T(8,128)}), f32[128,1,8,1,4096]{4,2,3,1,0:T(8,128)}, u32[]{:S(2)}, u32[]{:S(2)}) %all-to-all-start.1) | async-done | bytes 16777248 | tf_op jit(solution)/shard_map/all_to_all | solution.py:45
  334.4 17.7 %copy.104 = f32[128,1,8,1,4096]{4,0,2,3,1:T(8,128)} copy(f32[128,1,8,1,4096]{4,2,3,1,0:T(8,128)} %all-to-all-done.1) | data formatting | bytes 33554432 | tf_op jit(solution)/shard_map/all_to_all | solution.py:45
  352.2 7.1 %multiply_add_fusion = (f32[128,2,2,4096]{3,0,2,1:T(8,128)S(1)}, f32[128,2,2,4096]{3,0,2,1:T(8,128)S(1)}) fusion(f32[128,2,2,2,1,4096]{5,0,3,2,1,4:T(8,128)} %bitcast.135, f32[128,2]{0,1:T(2,128)S(1)} %get-tuple-element.21, f32[128,2]{0,1:T(2,128)S(1)} %get-tuple-element.20), kind=kLoop, calls=%fused_computation.15 | loop fusion | flops 12582912 | bytes 33556480 | tf_op jit(solution)/shard_map/add | solution.py:19
  359.3 10.0 %fusion.39 = f32[128,2,2,4096]{3,0,2,1:T(8,128)} fusion(f32[128,2,2,4096]{3,0,2,1:T(8,128)S(1)} %get-tuple-element.11), kind=kOutput, calls=%fused_computation.79 | convolution fusion | flops 3221454848 | bytes 16777216 | tf_op jit(solution)/shard_map/kp,prajc->krajc/dot_general | solution.py:62
  369.3 10.2 %fusion = f32[128,2,2,4096]{3,0,1,2:T(8,128)} fusion(f32[128,2,2,4096]{3,0,2,1:T(8,128)S(1)} %get-tuple-element.11), kind=kOutput, calls=%fused_computation.4 | convolution fusion | flops 3221454848 | bytes 16777216 | tf_op jit(solution)/shard_map/kp,prajc->krajc/dot_general | solution.py:62
  379.5 10.9 %convolution_add_fusion = f32[128,2,2,4096]{3,0,2,1:T(8,128)S(1)} fusion(f32[128,2,2,4096]{3,0,2,1:T(8,128)} %fusion.39, f32[128,2,2,4096]{3,0,2,1:T(8,128)S(1)} %get-tuple-element.10), kind=kOutput, calls=%fused_computation.18 | convolution fusion | flops 3223552000 | bytes 25165824 | tf_op jit(solution)/shard_map/kp,prajc->krajc/dot_general | solution.py:62
  390.4 16.9 %broadcast_multiply_fusion = (f32[128,2,2,4096]{3,0,1,2:T(8,128)}, f32[128,2,2,4096]{3,0,1,2:T(8,128)}) fusion(f32[128,2,2,4096]{3,0,2,1:T(8,128)S(1)} %convolution_add_fusion, f32[128,2,2,4096]{3,0,1,2:T(8,128)} %fusion, f32[128,2,2,4096]{3,0,2,1:T(8,128)} %copy-done), kind=kOutput, calls=%fused_computation.38 | convolution fusion | flops 3229843456 | bytes 41943040 | tf_op jit(solution)/shard_map/kp,prajc->krajc/dot_general | solution.py:62
  407.3 11.0 %fusion.4 = (f32[128,2,2,1,4096]{4,0,2,1,3:T(8,128)}, f32[128,2,2,4096]{3,0,2,1:T(8,128)}) fusion(f32[128,2,2,4096]{3,0,1,2:T(8,128)} %get-tuple-element.22, f32[128,2,2,4096]{3,0,2,1:T(8,128)S(1)} %convolution_add_fusion, f32[128,2,2,4096]{3,0,1,2:T(8,128)} %get-tuple-element.23), kind=kLoop, calls=%fused_computation.9 | loop fusion | flops 6291456 | bytes 41943040 | tf_op jit(solution)/shard_map/sub | solution.py:80
  418.4 9.6 %fusion.6 = f32[128,2,2,1,4096]{4,0,1,3,2:T(8,128)} fusion(f32[128,2,2,4096]{3,0,2,1:T(8,128)} %get-tuple-element.9, f32[128,2,2,4096]{3,0,1,2:T(8,128)} %get-tuple-element.23, f32[128,2,2,4096]{3,0,2,1:T(8,128)S(1)} %convolution_add_fusion), kind=kLoop, calls=%fused_computation.12 | loop fusion | flops 8388608 | bytes 33554432 | tf_op jit(solution)/shard_map/add | solution.py:79
  429.6 4.5 bitcast_add_fusion
  434.7 6.9 %fusion.18 = f32[2,4096,128]{2,1,0:T(8,128)S(1)} fusion(f32[128,2,4096]{2,0,1:T(8,128)S(1)} %fusion.13, f32[128,2,4096]{2,0,1:T(8,128)S(1)} %get-tuple-element.5), kind=kOutput, calls=%fused_computation.45 | convolution fusion | flops 1612939264 | bytes 12582912 | tf_op jit(solution)/shard_map/bk,krjc->rbjc/dot_general | solution.py:98
  441.6 7.1 %fusion.19 = f32[2,4096,128]{2,1,0:T(8,128)S(1)} fusion(f32[128,2,4096]{2,0,1:T(8,128)S(1)} %get-tuple-element.5, f32[128,2,4096]{2,0,1:T(8,128)S(1)} %fusion.13), kind=kOutput, calls=%fused_computation.46 | convolution fusion | flops 1612939264 | bytes 12582912 | tf_op jit(solution)/shard_map/bk,krjc->rbjc/dot_general | solution.py:98
  448.7 6.9 %fusion.10 = f32[2,1,4096,128]{3,2,0,1:T(8,128)S(1)} fusion(f32[2,4096,128]{2,1,0:T(8,128)S(1)} %fusion.19, f32[128,2,4096]{2,0,1:T(8,128)S(1)} %fusion.13, f32[128,2,4096]{2,0,1:T(8,128)S(1)} %get-tuple-element.5), kind=kOutput, calls=%fused_computation.20 | convolution fusion | flops 1613987840 | bytes 16777216 | tf_op jit(solution)/shard_map/bk,krjc->rbjc/dot_general | solution.py:98
  455.5 7.5 %subtract_bitcast_fusion = (f32[2,1,128,1,4096]{2,4,0,3,1:T(8,128)S(1)}, f32[2,1,128,1,4096]{2,4,0,3,1:T(8,128)S(1)}) fusion(f32[2,1,4096,128]{3,2,0,1:T(8,128)S(1)} %fusion.10, f32[2,128]{1,0:T(2,128)S(1)} %get-tuple-element.19, f32[2,128]{1,0:T(2,128)S(1)} %get-tuple-element.18, f32[2,4096,128]{2,1,0:T(8,128)S(1)} %fusion.18, ...), kind=kOutput, calls=%fused_computation.35 | convolution fusion | flops 1620279296 | bytes 25167872 | tf_op jit(solution)/shard_map/bk,krjc->rbjc/dot_general | solution.py:98
  463.1 3.8 pad_maximum_fusion
  466.8 9.0 %copy.121 = f32[2,2,128,1,4096]{4,2,1,0,3:T(8,128)} copy(f32[2,2,128,1,4096]{2,4,0,3,1:T(8,128)} %pad_maximum_fusion) | data formatting | bytes 16777216 | tf_op jit(solution)/shard_map/stack | solution.py:108
  475.8 12.0 %copy.122 = f32[1,4,128,4096]{3,1,0,2:T(4,128)} copy(f32[1,4,128,4096]{3,2,1,0:T(8,128)} %bitcast.137) | data formatting | bytes 16777216 | tf_op jit(solution)/shard_map/reshape | solution.py:108
  487.8 9.4 %all-to-all-start.2 = ((f32[1,4,128,4096]{3,1,0,2:T(4,128)}), f32[1,4,128,4096]{3,1,0,2:T(4,128)}, u32[]{:S(2)}, u32[]{:S(2)}) async-start(f32[1,4,128,4096]{3,1,0,2:T(4,128)} %copy.122), calls=%async_computation.2 | async-start | bytes 16777216 | tf_op jit(solution)/shard_map/all_to_all | solution.py:109
  498.0 102.8 %all-to-all-done.2 = f32[1,4,128,4096]{3,1,0,2:T(4,128)} async-done(((f32[1,4,128,4096]{3,1,0,2:T(4,128)}), f32[1,4,128,4096]{3,1,0,2:T(4,128)}, u32[]{:S(2)}, u32[]{:S(2)}) %all-to-all-start.2) | async-done | bytes 8388640 | tf_op jit(solution)/shard_map/all_to_all | solution.py:109
  600.8 10.0 %reshape.505 = f32[512,4096]{1,0:T(8,128)} reshape(f32[128,1,4,1,4096]{4,2,0,3,1:T(4,128)} %bitcast.37) | data formatting | bytes 16777216 | tf_op jit(solution)/shard_map/reshape | solution.py:113
  610.8 6.9 %fusion.12 = f32[128,1,1,4096]{3,0,2,1:T(8,128)S(1)} fusion(f32[128,512]{0,1:T(8,128)S(1)} %bitcast.139, f32[512,4096]{1,0:T(8,128)} %reshape.505), kind=kOutput, calls=%fused_computation.24 | convolution fusion | flops 3221749760 | bytes 10747904 | tf_op jit(solution)/shard_map/dot_general | solution.py:114
  617.7 2.2 copy.123
  619.9 40.5 %all_to_all.48 = f32[128,1,1,4096]{3,2,1,0:T(1,128)S(1)} all-to-all(f32[128,1,1,4096]{3,2,1,0:T(1,128)S(1)} %copy.123), channel_id=1, replica_groups=mesh['outer'=8,'inner'=16] {'outer','inner'}, dimensions={0} | all-to-all | bytes 4194304 | tf_op jit(solution)/shard_map/all_to_all | solution.py:116
  660.4 2.9 fusion.16
  (29 shorter events, 7.5 us)
Async XLA Ops:
  6.7 41.5 %all-to-all-start = ((bf16[1,2,128,4096]{3,1,0,2:T(2,128)(2,1)}), bf16[1,2,128,4096]{3,1,0,2:T(2,128)(2,1)}, u32[]{:S(2)}, u32[]{:S(2)}) async-start(bf16[1,2,128,4096]{3,1,0,2:T(2,128)(2,1)} %copy.100), calls=%async_computation | async-start | bytes 4194304 | tf_op jit(solution)/shard_map/all_to_all | solution.py:37
  18.4 0.5 copy-start.6
  97.8 236.7 %all-to-all-start.1 = ((f32[128,1,8,1,4096]{4,2,3,1,0:T(8,128)}), f32[128,1,8,1,4096]{4,2,3,1,0:T(8,128)}, u32[]{:S(2)}, u32[]{:S(2)}) async-start(f32[128,1,8,1,4096]{4,2,3,1,0:T(8,128)} %copy.103), calls=%async_computation.1 | async-start | bytes 33554432 | tf_op jit(solution)/shard_map/all_to_all | solution.py:45
  359.3 20.3 %copy-start = (f32[128,2,2,4096]{3,0,2,1:T(8,128)}, f32[128,2,2,4096]{3,0,2,1:T(8,128)S(1)}, u32[]{:S(2)}) copy-start(f32[128,2,2,4096]{3,0,2,1:T(8,128)S(1)} %get-tuple-element.10) | copy-start | bytes 25165828
  418.4 11.3 %copy-start.1 = (f32[128,2,2,1,4096]{4,0,2,1,3:T(8,128)S(1)}, f32[128,2,2,1,4096]{4,0,2,1,3:T(8,128)}, u32[]{:S(2)}) copy-start(f32[128,2,2,1,4096]{4,0,2,1,3:T(8,128)} %get-tuple-element.8) | copy-start | bytes 25165828
  487.8 9.4 %copy-start.7 = (s32[128]{0:T(128)S(1)}, s32[128]{0:T(128)}, u32[]{:S(2)}) copy-start(s32[128]{0:T(128)} %copy-done.6) | copy-start | bytes 1540
  487.8 113.0 %all-to-all-start.2 = ((f32[1,4,128,4096]{3,1,0,2:T(4,128)}), f32[1,4,128,4096]{3,1,0,2:T(4,128)}, u32[]{:S(2)}, u32[]{:S(2)}) async-start(f32[1,4,128,4096]{3,1,0,2:T(4,128)} %copy.122), calls=%async_computation.2 | async-start | bytes 16777216 | tf_op jit(solution)/shard_map/all_to_all | solution.py:109
  617.7 42.7 %copy-start.2 = (bf16[128,4096]{1,0:T(8,128)(2,1)S(1)}, bf16[128,4096]{1,0:T(8,128)(2,1)}, u32[]{:S(2)}) copy-start(bf16[128,4096]{1,0:T(8,128)(2,1)} %param.6) | copy-start | bytes 3145732
  617.7 42.7 %copy-start.3 = (bf16[128,4096]{1,0:T(8,128)(2,1)S(1)}, bf16[128,4096]{1,0:T(8,128)(2,1)}, u32[]{:S(2)}) copy-start(bf16[128,4096]{1,0:T(8,128)(2,1)} %param.5) | copy-start | bytes 3145732
  617.7 42.7 %copy-start.4 = (bf16[128,4096]{1,0:T(8,128)(2,1)S(1)}, bf16[128,4096]{1,0:T(8,128)(2,1)}, u32[]{:S(2)}) copy-start(bf16[128,4096]{1,0:T(8,128)(2,1)} %param.7) | copy-start | bytes 3145732
  617.7 42.7 %copy-start.5 = (f32[4096]{0:T(1024)S(1)}, f32[4096]{0:T(1024)}, u32[]{:S(2)}) copy-start(f32[4096]{0:T(1024)} %param.9) | copy-start | bytes 49156
where the time goes:
time: 673 us; the launch traced here: 663 us
  waiting for transfers between devices  362 us (54%)
  local copies, waits for them, and re-layouts  96.7 us (14%)
  matrix products  92.8 us (14%)
  other arithmetic  44.1 us (7%)
  blocking collectives  40.5 us (6%)
  starting transfers between devices  27.4 us (4%)
    all_to_all x1, waiting for transfers between devices, shards(): lax.all_to_all(cross_rows, ('outer', 'inner'), split_axis=0, concat_axis=...  230 us
    all_to_all x1, waiting for transfers between devices, shards(): lax.all_to_all(leaving, ('outer', 'inner'), split_axis=2, concat_axis=0,...  103 us
    dot_general x4, matrix products, over_rows(): return jnp.einsum('kp,prajc->krajc', matrix, values, precision=highest)  48 us
    all_to_all x1, blocking collectives, shards(): lax.all_to_all(partial_rows, ('outer', 'inner'), split_axis=0, concat_axi...  40.5 us
    all_to_all x1, waiting for transfers between devices, shards(): lax.all_to_all(stacked, ('outer', 'inner'), split_axis=2, concat_axis=0,...  28.6 us
    dot_general x4, matrix products, back_rows(): return jnp.einsum('bk,krjc->rbjc', matrix, values, precision=highest)  28.3 us
    all_to_all x1, local copies, waits for them, and re-layouts, shards(): lax.all_to_all(cross_rows, ('outer', 'inner'), split_axis=0, concat_axis=...  17.7 us
    reshape x1, local copies, waits for them, and re-layouts, shards(): cross_rows = cross_rows.reshape(groups, 1, 8, slab_rows, channels)  17.7 us
  transfers between devices with their start and end apart: 3, of which 3 were waited for; matrix products, arithmetic and copies ran while one was open for 0% of the time, Pallas kernels for 0%

commit v1 on v0

v1 whole, which is shorter than its diff:
```python
import functools
import math

import jax
import jax.numpy as jnp
import numpy as np
from jax import lax
from jax.experimental import pallas as pl
from jax.experimental.pallas import tpu as pltpu
from jax.sharding import PartitionSpec as P

MESH = pl.DeviceIdType.MESH
DEVICES = 128
BLOCK = 128
CHUNKS = 2
SHARE = 16
GROUPS = 16
MEMBERS = 8
BF, F32 = jnp.bfloat16, jnp.float32


def tables():
    total = DEVICES * BLOCK
    place = np.arange(128)
    shifted = place + 0.25
    phi = 2.0 * math.pi * np.outer(shifted, place) / 128
    tau = 2.0 * math.pi * np.outer(shifted, place) / total
    psi = 2.0 * math.pi * np.outer(place, place) / 128
    c, s = np.cos(psi), np.sin(psi)
    first = np.concatenate([np.cos(phi), -np.sin(phi)], 0)
    second = np.block([[c, -s], [s, c]])
    second_back = np.block([[c, s], [-s, c]])
    first_back = np.concatenate([np.cos(phi).T, -np.sin(phi).T], 1) / total
    return (
        jnp.asarray(first, BF),
        jnp.asarray(np.cos(tau), F32),
        jnp.asarray(-np.sin(tau), F32),
        jnp.asarray(second, BF),
        jnp.asarray(second_back, BF),
        jnp.asarray(first_back, BF),
    )


def dot(a, b):
    return jnp.dot(a, b, preferred_element_type=F32)


def kernel(
    gate_hbm, value_hbm, gout_hbm, filt_hbm, skip_ref, f1, tr_ref, ti_ref, f2, f2b, f1b, out_hbm,
    gate, value, gout, filt, outv, send, recv, wide, owide, osend, orecv,
    load_sem, store_sem, self_sem, in_send, in_recv, out_send, out_recv,
):
    half = GROUPS * 128
    outer, inner = lax.axis_index("outer"), lax.axis_index("inner")
    me = outer * 16 + inner
    x0, z0 = outer // 2, lax.rem(outer, 2) + 2 * (inner // 8)
    y0, c0 = lax.rem(inner // 2, 4), lax.rem(inner, 2)
    u0, v0 = lax.rem(y0 + 4 - x0, 4), lax.rem(z0 + 4 - x0, 4)
    my_group, my_member = u0 * 4 + v0, x0 * 2 + c0

    barrier = pltpu.get_barrier_semaphore()

    def greet(i, carry):
        d = lax.rem(me + i, DEVICES)
        pl.semaphore_signal(barrier, inc=1, device_id=(d // 16, lax.rem(d, 16)), device_id_type=MESH)
        return carry

    loads = []
    for k in range(CHUNKS):
        lanes = pl.ds(k * half, half)
        loads.append([
            pltpu.make_async_copy(src.at[:, lanes], dst.at[:, lanes], load_sem.at[k, n])
            for n, (src, dst) in enumerate([(gate_hbm, gate), (value_hbm, value), (filt_hbm, filt)])
        ])
        for copy in loads[k]:
            copy.start()
    gout_load = pltpu.make_async_copy(gout_hbm, gout, load_sem.at[0, 3])
    gout_load.start()
    lax.fori_loop(1, DEVICES, greet, 0)

    def group_at(step):
        u, v = lax.rem(u0 + step // 4, 4), lax.rem(v0 + step, 4)
        return u, v, u * 4 + v

    def partner(u, v, n):
        x, c = lax.rem(x0 + n // 2, 4), lax.rem(c0 + n, 2)
        y, z = lax.rem(x + u, 4), lax.rem(x + v, 4)
        return (x * 2 + lax.rem(z, 2), (z // 2) * 8 + y * 2 + c), x * 2 + c

    def prepare(k, step):
        _, _, g = group_at(step)
        lanes = pl.ds(pl.multiple_of(k * half + g * 128, 128), 128)
        signal = (gate[:, lanes].astype(F32) * value[:, lanes].astype(F32)).astype(BF)
        send[k, g, :, 0] = signal.T.reshape(MEMBERS, SHARE, BLOCK)
        send[k, g, :, 1] = filt[:, lanes].T.reshape(MEMBERS, SHARE, BLOCK)

    def ship_in(k, step, first):
        u, v, g = group_at(step)
        for n in range(first, MEMBERS):
            where, m = partner(u, v, n)
            pltpu.make_async_remote_copy(
                src_ref=send.at[k, g, m], dst_ref=recv.at[k, me], send_sem=in_send.at[k],
                recv_sem=in_recv.at[k], device_id=where, device_id_type=MESH,
            ).start()

    def ship_out(k, step, first):
        u, v, _ = group_at(step)
        for n in range(first, MEMBERS):
            where, _ = partner(u, v, n)
            pltpu.make_async_remote_copy(
                src_ref=osend.at[k, where[0] * 16 + where[1]], dst_ref=orecv.at[k, my_group, my_member],
                send_sem=out_send.at[k], recv_sem=out_recv.at[k], device_id=where, device_id_type=MESH,
            ).start()

    def all_in(k):
        part = pl.ds(0, DEVICES - 1)
        return pltpu.make_async_remote_copy(
            src_ref=recv.at[k, part], dst_ref=recv.at[k, part], send_sem=in_send.at[k], recv_sem=in_recv.at[k],
            device_id=(outer, inner), device_id_type=MESH,
        )

    def all_out(k):
        part = pl.ds(0, DEVICES - 1)
        return pltpu.make_async_remote_copy(
            src_ref=osend.at[k, part], dst_ref=osend.at[k, part], send_sem=out_send.at[k],
            recv_sem=out_recv.at[k], device_id=(outer, inner), device_id_type=MESH,
        )

    def loop(start, stop, body, unroll=1):
        def step(i, carry):
            body(i)
            return carry

        lax.fori_loop(start, stop, step, 0, unroll=unroll)

    def convolve(k):
        def widen(i):
            rows = pl.ds(pl.multiple_of(i * 256, 256), 256)
            wide[rows, :] = recv[k, pl.ds(i * 8, 8)].astype(F32).reshape(256, BLOCK)

        loop(0, DEVICES // 8, widen, unroll=2)

        def channel(i):
            pair = [
                wide[pl.ds(arr * SHARE + i * 2 + e, DEVICES, stride=2 * SHARE), :].astype(BF)
                for e in range(2)
                for arr in range(2)
            ]
            spread = dot(f1[...], jnp.concatenate(pair, axis=1))
            tr, ti = tr_ref[...], ti_ref[...]
            rows = []
            for n in range(4):
                re, im = spread[:128, n * 128 : n * 128 + 128], spread[128:, n * 128 : n * 128 + 128]
                rows.append(jnp.concatenate([re * tr - im * ti, re * ti + im * tr], axis=1).astype(BF))
            spectra = dot(jnp.concatenate(rows, axis=0), f2[...])
            rows = []
            for e in range(2):
                sig, res = spectra[e * 256 : e * 256 + 128], spectra[e * 256 + 128 : e * 256 + 256]
                sr, si, hr, hi = sig[:, :128], sig[:, 128:], res[:, :128], res[:, 128:]
                rows.append(jnp.concatenate([sr * hr - si * hi, sr * hi + si * hr], axis=1).astype(BF))
            back = dot(jnp.concatenate(rows, axis=0), f2b[...])
            columns = []
            for e in range(2):
                re, im = back[e * 128 : e * 128 + 128, :128], back[e * 128 : e * 128 + 128, 128:]
                columns.append(jnp.concatenate([re * tr + im * ti, im * tr - re * ti], axis=0).astype(BF))
            result = dot(f1b[...], jnp.concatenate(columns, axis=1))
            for e in range(2):
                owide[pl.ds(i * 2 + e, DEVICES, stride=SHARE), :] = result[:, e * 128 : e * 128 + 128]

        loop(0, SHARE // 2, channel)

        def narrow(i):
            rows = pl.ds(pl.multiple_of(i * 256, 256), 256)
            osend[k, pl.ds(i * 16, 16)] = owide[rows, :].reshape(16, SHARE, BLOCK).astype(BF)

        loop(0, DEVICES // 16, narrow, unroll=2)

    def finish(k, g):
        lanes = pl.ds(pl.multiple_of(k * half + g * 128, 128), 128)
        convolved = orecv[k, g].reshape(128, BLOCK).T.astype(F32)
        signal = (gate[:, lanes].astype(F32) * value[:, lanes].astype(F32)).astype(BF).astype(F32)
        result = gout[:, lanes].astype(F32) * (convolved + skip_ref[:, lanes] * signal)
        outv[:, lanes] = result.astype(BF)

    own_in = [
        pltpu.make_async_copy(send.at[k, my_group, my_member], recv.at[k, me], self_sem.at[0, k])
        for k in range(CHUNKS)
    ]
    own_out = [
        pltpu.make_async_copy(osend.at[k, me], orecv.at[k, my_group, my_member], self_sem.at[1, k])
        for k in range(CHUNKS)
    ]
    for k in range(CHUNKS):
        for copy in loads[k]:
            copy.wait()
        loop(0, GROUPS, functools.partial(prepare, k), unroll=2)
        if k == 0:
            pl.semaphore_wait(barrier, DEVICES - 1)
        ship_in(k, 0, 1)
        loop(1, GROUPS, lambda step: ship_in(k, step, 0))
        own_in[k].start()
    for k in range(CHUNKS):
        all_in(k).wait_recv()
        own_in[k].wait()
        convolve(k)
        ship_out(k, 0, 1)
        loop(1, GROUPS, lambda step: ship_out(k, step, 0))
        own_out[k].start()
    gout_load.wait()
    stores = []
    for k in range(CHUNKS):
        all_out(k).wait_recv()
        own_out[k].wait()
        loop(0, GROUPS, functools.partial(finish, k), unroll=2)
        lanes = pl.ds(k * half, half)
        stores.append(pltpu.make_async_copy(outv.at[:, lanes], out_hbm.at[:, lanes], store_sem.at[k]))
        stores[k].start()
    for k in range(CHUNKS):
        all_in(k).wait_send()
        all_out(k).wait_send()
        stores[k].wait()


def shards(gate_in, value_in, gate_out, filters, skip_bias):
    rows, channels = gate_in.shape
    any_spec = pl.BlockSpec(memory_space=pl.ANY)
    vmem_spec = pl.BlockSpec(memory_space=pltpu.VMEM)
    full = pltpu.VMEM((rows, channels), BF)
    dma = pltpu.SemaphoreType.DMA
    return pl.pallas_call(
        kernel,
        out_shape=jax.ShapeDtypeStruct((rows, channels), BF),
        in_specs=[any_spec] * 4 + [vmem_spec] * 7,
        out_specs=any_spec,
        scratch_shapes=[
            full, full, full, full, full,
            pltpu.VMEM((CHUNKS, GROUPS, MEMBERS, 2, SHARE, BLOCK), BF),
            pltpu.VMEM((CHUNKS, DEVICES, 2, SHARE, BLOCK), BF),
            pltpu.VMEM((DEVICES * 2 * SHARE, BLOCK), F32),
            pltpu.VMEM((DEVICES * SHARE, BLOCK), F32),
            pltpu.VMEM((CHUNKS, DEVICES, SHARE, BLOCK), BF),
            pltpu.VMEM((CHUNKS, GROUPS, MEMBERS, SHARE, BLOCK), BF),
            dma((CHUNKS, 4)), dma((CHUNKS,)), dma((2, CHUNKS)),
            dma((CHUNKS,)), dma((CHUNKS,)), dma((CHUNKS,)), dma((CHUNKS,)),
        ],
        compiler_params=pltpu.CompilerParams(collective_id=0, has_side_effects=True, vmem_limit_bytes=40 * 2**20),
        name="gated_convolution",
    )(gate_in, value_in, gate_out, filters, skip_bias.reshape(1, channels), *tables())


def solution(mesh):
    spread = P(("outer", "inner"), None)
    return jax.shard_map(
        shards, mesh=mesh, in_specs=(spread,) * 4 + (P(),), out_specs=spread, check_vma=False
    )
```

time: 673 us -> 71.2 us (0.11); the launches traced: 663 us -> 70 us
  waiting for transfers between devices: 362 us -> 0 us
  matrix products: 92.8 us -> 0 us
  local copies, waits for them, and re-layouts: 96.7 us -> 11.7 us
  Pallas kernels: 0 us -> 58.2 us
  other arithmetic: 44.1 us -> 0 us
  blocking collectives: 40.5 us -> 0 us
  starting transfers between devices: 27.4 us -> 0 us
    all_to_all x3 -> x0, waiting for transfers between devices: 362 us -> none  [the longest x1 230 us: shards(): lax.all_to_all(cross_rows, ('outer', 'inner'), split_axis=0, concat_axis=...]
    dot_general x10 -> x0, matrix products: 92.8 us -> none  [the longest x4 48 us: over_rows(): return jnp.einsum('kp,prajc->krajc', matrix, values, precision=highest)]
    pallas_call x0 -> x1, Pallas kernels: none -> 58.2 us  [shards(): pl.pallas_call(kernel, out_shape=jax.ShapeDtypeStruct((rows, channels), B...]
    reshape x4 -> x0, local copies, waits for them, and re-layouts: 41.8 us -> none  [the longest x1 17.7 us: shards(): cross_rows = cross_rows.reshape(groups, 1, 8, slab_rows, channels)]
    all_to_all x1 -> x0, blocking collectives: 40.5 us -> none  [shards(): lax.all_to_all(partial_rows, ('outer', 'inner'), split_axis=0, concat_axi...]
    all_to_all x3 -> x0, starting transfers between devices: 27.4 us -> none  [the longest x1 11.7 us: shards(): lax.all_to_all(stacked, ('outer', 'inner'), split_axis=2, concat_axis=0,...]
    all_to_all x2 -> x0, local copies, waits for them, and re-layouts: 22.6 us -> none  [the longest x1 17.7 us: shards(): lax.all_to_all(cross_rows, ('outer', 'inner'), split_axis=0, concat_axis=...]
    add x6 -> x0, other arithmetic: 21.3 us -> none  [the longest x1 9.63 us: shards(): spec_real = over_slab(cos_slab, turn_real) + over_slab(sin_slab, turn_imag)]
  transfers between devices with their start and end apart: 3 -> 0, of which waited for: 3 -> 0; matrix products, arithmetic and copies ran while one was open for 0% -> 0% of each run, Pallas kernels for 0% -> 0%
where the time goes in v1:
time: 71.2 us; the launch traced here: 70 us
  Pallas kernels  58.2 us (82%)
  local copies, waits for them, and re-layouts  11.7 us (16%)
    pallas_call x1, Pallas kernels, shards(): pl.pallas_call(kernel, out_shape=jax.ShapeDtypeStruct((rows, channels), B...  58.2 us
    unnamed x23, local copies, waits for them, and re-layouts  11.7 us

profile of v1, /device:TPU:0, one launch (start us, length us, event | category | flops | bytes accessed | tf_op | source)
XLA Modules:
  0.0 70.0 jit_solution(818105937875839760)
XLA Ops:
  0.0 0.0 copy-start
  0.0 1.2 %copy-done = bf16[128,4096]{1,0:T(8,128)(2,1)S(1)} copy-done((bf16[128,4096]{1,0:T(8,128)(2,1)S(1)}, bf16[128,4096]{1,0:T(8,128)(2,1)}, u32[]{:S(2)}) %copy-start) | copy-done | bytes 1048600
  1.2 0.0 copy-start.1
  1.2 1.2 %copy-done.1 = bf16[128,4096]{1,0:T(8,128)(2,1)S(1)} copy-done((bf16[128,4096]{1,0:T(8,128)(2,1)S(1)}, bf16[128,4096]{1,0:T(8,128)(2,1)}, u32[]{:S(2)}) %copy-start.1) | copy-done | bytes 1048600
  2.5 0.0 copy-start.2
  2.5 1.2 %copy-done.2 = bf16[128,4096]{1,0:T(8,128)(2,1)S(1)} copy-done((bf16[128,4096]{1,0:T(8,128)(2,1)S(1)}, bf16[128,4096]{1,0:T(8,128)(2,1)}, u32[]{:S(2)}) %copy-start.2) | copy-done | bytes 1048600
  3.7 0.0 copy-start.3
  3.7 1.2 %copy-done.3 = bf16[128,4096]{1,0:T(8,128)(2,1)S(1)} copy-done((bf16[128,4096]{1,0:T(8,128)(2,1)S(1)}, bf16[128,4096]{1,0:T(8,128)(2,1)}, u32[]{:S(2)}) %copy-start.3) | copy-done | bytes 1048600
  4.9 0.0 copy-start.4
  4.9 0.9 %copy-done.4 = bf16[256,256]{1,0:T(8,128)(2,1)S(1)} copy-done((bf16[256,256]{1,0:T(8,128)(2,1)S(1)}, bf16[256,256]{1,0:T(8,128)(2,1)}, u32[]{:S(2)}) %copy-start.4) | copy-done | bytes 131096
  5.8 0.0 copy-start.5
  5.8 0.9 %copy-done.5 = bf16[256,256]{1,0:T(8,128)(2,1)S(1)} copy-done((bf16[256,256]{1,0:T(8,128)(2,1)S(1)}, bf16[256,256]{1,0:T(8,128)(2,1)}, u32[]{:S(2)}) %copy-start.5) | copy-done | bytes 131096
  6.7 0.0 copy-start.6
  6.7 0.8 %copy-done.6 = bf16[128,256]{1,0:T(8,128)(2,1)S(1)} copy-done((bf16[128,256]{1,0:T(8,128)(2,1)S(1)}, bf16[128,256]{1,0:T(8,128)(2,1)}, u32[]{:S(2)}) %copy-start.6) | copy-done | bytes 65560
  7.6 0.0 copy-start.7
  7.6 0.8 %copy-done.7 = f32[128,128]{1,0:T(8,128)S(1)} copy-done((f32[128,128]{1,0:T(8,128)S(1)}, f32[128,128]{1,0:T(8,128)}, u32[]{:S(2)}) %copy-start.7) | copy-done | bytes 65560
  8.4 0.0 copy-start.8
  8.4 0.8 %copy-done.8 = f32[128,128]{1,0:T(8,128)S(1)} copy-done((f32[128,128]{1,0:T(8,128)S(1)}, f32[128,128]{1,0:T(8,128)}, u32[]{:S(2)}) %copy-start.8) | copy-done | bytes 65560
  9.2 0.0 copy-start.9
  9.2 0.8 %copy-done.9 = bf16[256,128]{1,0:T(8,128)(2,1)S(1)} copy-done((bf16[256,128]{1,0:T(8,128)(2,1)S(1)}, bf16[256,128]{1,0:T(8,128)(2,1)}, u32[]{:S(2)}) %copy-start.9) | copy-done | bytes 65560
  10.1 0.0 copy-start.10
  10.1 0.7 %copy-done.10 = f32[4096]{0:T(1024)S(1)} copy-done((f32[4096]{0:T(1024)S(1)}, f32[4096]{0:T(1024)}, u32[]{:S(2)}) %copy-start.10) | copy-done | bytes 16408
  10.8 58.2 %gated_convolution.1 = bf16[128,4096]{1,0:T(8,128)(2,1)S(1)} custom-call(bf16[128,4096]{1,0:T(8,128)(2,1)S(1)} %copy-done, bf16[128,4096]{1,0:T(8,128)(2,1)S(1)} %copy-done.1, bf16[128,4096]{1,0:T(8,128)(2,1)S(1)} %copy-done.2, bf16[128,4096]{1,0:T(8,128)(2,1)S(1)} %copy-done.3, f32[1,4096]{1,0:T(1,128)S(1)} %bitcast.1, bf16[256,128]{1,0:T(8,128)(2,1)S(1)} %copy-done.9, ...), custom_call_target="tpu_custom_call" | custom-call | tf_op jit(solution)/shard_map/gated_convolution/pallas_call | solution.py:230
  69.0 1.0 %copy.13 = bf16[128,4096]{1,0:T(8,128)(2,1)} copy(bf16[128,4096]{1,0:T(8,128)(2,1)S(1)} %gated_convolution.1) | data formatting | bytes 2097152
Async XLA Ops:
  0.0 1.2 %copy-start = (bf16[128,4096]{1,0:T(8,128)(2,1)S(1)}, bf16[128,4096]{1,0:T(8,128)(2,1)}, u32[]{:S(2)}) copy-start(bf16[128,4096]{1,0:T(8,128)(2,1)} %gate_hbm.1) | copy-start | bytes 3145732
  1.2 1.2 %copy-start.1 = (bf16[128,4096]{1,0:T(8,128)(2,1)S(1)}, bf16[128,4096]{1,0:T(8,128)(2,1)}, u32[]{:S(2)}) copy-start(bf16[128,4096]{1,0:T(8,128)(2,1)} %value_hbm.1) | copy-start | bytes 3145732
  2.5 1.2 %copy-start.2 = (bf16[128,4096]{1,0:T(8,128)(2,1)S(1)}, bf16[128,4096]{1,0:T(8,128)(2,1)}, u32[]{:S(2)}) copy-start(bf16[128,4096]{1,0:T(8,128)(2,1)} %gout_hbm.1) | copy-start | bytes 3145732
  3.7 1.2 %copy-start.3 = (bf16[128,4096]{1,0:T(8,128)(2,1)S(1)}, bf16[128,4096]{1,0:T(8,128)(2,1)}, u32[]{:S(2)}) copy-start(bf16[128,4096]{1,0:T(8,128)(2,1)} %filt_hbm.1) | copy-start | bytes 3145732
  4.9 0.9 %copy-start.4 = (bf16[256,256]{1,0:T(8,128)(2,1)S(1)}, bf16[256,256]{1,0:T(8,128)(2,1)}, u32[]{:S(2)}) copy-start(bf16[256,256]{1,0:T(8,128)(2,1)} %constant.16.clone.f2b) | copy-start | bytes 393220
  5.8 0.9 %copy-start.5 = (bf16[256,256]{1,0:T(8,128)(2,1)S(1)}, bf16[256,256]{1,0:T(8,128)(2,1)}, u32[]{:S(2)}) copy-start(bf16[256,256]{1,0:T(8,128)(2,1)} %constant.15.clone.f2) | copy-start | bytes 393220
  6.7 0.8 %copy-start.6 = (bf16[128,256]{1,0:T(8,128)(2,1)S(1)}, bf16[128,256]{1,0:T(8,128)(2,1)}, u32[]{:S(2)}) copy-start(bf16[128,256]{1,0:T(8,128)(2,1)} %constant.17.clone.f1b) | copy-start | bytes 196612
  7.6 0.8 %copy-start.7 = (f32[128,128]{1,0:T(8,128)S(1)}, f32[128,128]{1,0:T(8,128)}, u32[]{:S(2)}) copy-start(f32[128,128]{1,0:T(8,128)} %constant.14.clone.ti_ref) | copy-start | bytes 196612
  8.4 0.8 %copy-start.8 = (f32[128,128]{1,0:T(8,128)S(1)}, f32[128,128]{1,0:T(8,128)}, u32[]{:S(2)}) copy-start(f32[128,128]{1,0:T(8,128)} %constant.13.clone.tr_ref) | copy-start | bytes 196612
  9.2 0.8 %copy-start.9 = (bf16[256,128]{1,0:T(8,128)(2,1)S(1)}, bf16[256,128]{1,0:T(8,128)(2,1)}, u32[]{:S(2)}) copy-start(bf16[256,128]{1,0:T(8,128)(2,1)} %constant.12.clone.f1) | copy-start | bytes 196612
  10.1 0.7 %copy-start.10 = (f32[4096]{0:T(1024)S(1)}, f32[4096]{0:T(1024)}, u32[]{:S(2)}) copy-start(f32[4096]{0:T(1024)} %param.15) | copy-start | bytes 49156

commit v2 on v1

--- a/solution.py
+++ b/solution.py
@@ -31,14 +31,9 @@
     second = np.block([[c, -s], [s, c]])
     second_back = np.block([[c, s], [-s, c]])
     first_back = np.concatenate([np.cos(phi).T, -np.sin(phi).T], 1) / total
-    return (
-        jnp.asarray(first, BF),
-        jnp.asarray(np.cos(tau), F32),
-        jnp.asarray(-np.sin(tau), F32),
-        jnp.asarray(second, BF),
-        jnp.asarray(second_back, BF),
-        jnp.asarray(first_back, BF),
-    )
+    square = np.concatenate([second, second_back, first_back, np.pad(first, ((0, 0), (0, 128)))], 0)
+    turn = np.stack([np.cos(tau), -np.sin(tau)])
+    return jnp.asarray(square, BF), jnp.asarray(turn, F32)
 
 
 def dot(a, b):
@@ -46,9 +41,9 @@
 
 
 def kernel(
-    gate_hbm, value_hbm, gout_hbm, filt_hbm, skip_ref, f1, tr_ref, ti_ref, f2, f2b, f1b, out_hbm,
-    gate, value, gout, filt, outv, send, recv, wide, owide, osend, orecv,
-    load_sem, store_sem, self_sem, in_send, in_recv, out_send, out_recv,
+    gate_hbm, value_hbm, gout_hbm, filt_hbm, skip_hbm, square_hbm, turn_hbm, out_hbm,
+    gate, value, gout, filt, skip_ref, square, turn, outv, send, recv, wide, owide, turned, product, unturned, osend, orecv,
+    load_sem, late_sem, store_sem, self_sem, in_send, in_recv, out_send, out_recv, core_sem, y_sem, z_sem,
 ):
     half = GROUPS * 128
     outer, inner = lax.axis_index("outer"), lax.axis_index("inner")
@@ -60,10 +55,19 @@
 
     barrier = pltpu.get_barrier_semaphore()
 
-    def greet(i, carry):
-        d = lax.rem(me + i, DEVICES)
-        pl.semaphore_signal(barrier, inc=1, device_id=(d // 16, lax.rem(d, 16)), device_id_type=MESH)
-        return carry
+    def place(x, y, z, c):
+        return x * 2 + lax.rem(z, 2), (z // 2) * 8 + y * 2 + c
+
+    along_x = [place(lax.rem(x0 + n, 4), y0, z0, c0) for n in range(1, 4)]
+    along_y = [place(x0, lax.rem(y0 + n, 4), z0, c0) for n in range(1, 4)]
+    along_z = [place(x0, y0, lax.rem(z0 + n, 4), c0) for n in range(1, 4)]
+    other_core = [place(x0, y0, z0, 1 - c0)]
+
+    def greet(sem, devices):
+        for where in devices:
+            pl.semaphore_signal(sem, inc=1, device_id=where, device_id_type=MESH)
+
+    greet(barrier, along_x + along_y + along_z + other_core)
 
     loads = []
     for k in range(CHUNKS):
@@ -74,9 +78,14 @@
         ])
         for copy in loads[k]:
             copy.start()
-    gout_load = pltpu.make_async_copy(gout_hbm, gout, load_sem.at[0, 3])
-    gout_load.start()
-    lax.fori_loop(1, DEVICES, greet, 0)
+    late = [
+        pltpu.make_async_copy(src, dst, late_sem.at[n])
+        for n, (src, dst) in enumerate([
+            (square_hbm, square), (turn_hbm, turn), (skip_hbm, skip_ref), (gout_hbm, gout)
+        ])
+    ]
+    for copy in late:
+        copy.start()
 
     def group_at(step):
         u, v = lax.rem(u0 + step // 4, 4), lax.rem(v0 + step, 4)
@@ -140,34 +149,61 @@
 
         loop(0, DEVICES // 8, widen, unroll=2)
 
-        def channel(i):
+        def stage_first(i):
             pair = [
                 wide[pl.ds(arr * SHARE + i * 2 + e, DEVICES, stride=2 * SHARE), :].astype(BF)
                 for e in range(2)
                 for arr in range(2)
             ]
-            spread = dot(f1[...], jnp.concatenate(pair, axis=1))
-            tr, ti = tr_ref[...], ti_ref[...]
-            rows = []
+            spread = dot(square[640:896, :128], jnp.concatenate(pair, axis=1))
+            tr, ti = turn[0], turn[1]
             for n in range(4):
                 re, im = spread[:128, n * 128 : n * 128 + 128], spread[128:, n * 128 : n * 128 + 128]
-                rows.append(jnp.concatenate([re * tr - im * ti, re * ti + im * tr], axis=1).astype(BF))
-            spectra = dot(jnp.concatenate(rows, axis=0), f2[...])
-            rows = []
+                turned[n * 128 : n * 128 + 128, :128] = (re * tr - im * ti).astype(BF)
+                turned[n * 128 : n * 128 + 128, 128:] = (re * ti + im * tr).astype(BF)
+
+        def stage_product():
+            spectra = dot(turned[...], square[0:256, :])
             for e in range(2):
                 sig, res = spectra[e * 256 : e * 256 + 128], spectra[e * 256 + 128 : e * 256 + 256]
                 sr, si, hr, hi = sig[:, :128], sig[:, 128:], res[:, :128], res[:, 128:]
-                rows.append(jnp.concatenate([sr * hr - si * hi, sr * hi + si * hr], axis=1).astype(BF))
-            back = dot(jnp.concatenate(rows, axis=0), f2b[...])
-            columns = []
+                product[e * 128 : e * 128 + 128, :128] = (sr * hr - si * hi).astype(BF)
+                product[e * 128 : e * 128 + 128, 128:] = (sr * hi + si * hr).astype(BF)
+
+        def stage_back():
+            back = dot(product[...], square[256:512, :])
+            tr, ti = turn[0], turn[1]
             for e in range(2):
                 re, im = back[e * 128 : e * 128 + 128, :128], back[e * 128 : e * 128 + 128, 128:]
-                columns.append(jnp.concatenate([re * tr + im * ti, im * tr - re * ti], axis=0).astype(BF))
-            result = dot(f1b[...], jnp.concatenate(columns, axis=1))
+                unturned[:128, e * 128 : e * 128 + 128] = (re * tr + im * ti).astype(BF)
+                unturned[128:, e * 128 : e * 128 + 128] = (im * tr - re * ti).astype(BF)
+
+        def stage_last(i):
+            result = dot(square[512:640, :], unturned[...])
             for e in range(2):
                 owide[pl.ds(i * 2 + e, DEVICES, stride=SHARE), :] = result[:, e * 128 : e * 128 + 128]
 
-        loop(0, SHARE // 2, channel)
+        pairs = SHARE // 2
+        stage_first(0)
+        stage_product()
+        stage_first(1)
+        stage_back()
+        stage_product()
+        stage_first(2)
+
+        def steady(i):
+            stage_last(i)
+            stage_back()
+            stage_product()
+            stage_first(i + 3)
+
+        loop(0, pairs - 3, steady)
+        stage_last(pairs - 3)
+        stage_back()
+        stage_product()
+        stage_last(pairs - 2)
+        stage_back()
+        stage_last(pairs - 1)
 
         def narrow(i):
             rows = pl.ds(pl.multiple_of(i * 256, 256), 256)
@@ -195,18 +231,24 @@
             copy.wait()
         loop(0, GROUPS, functools.partial(prepare, k), unroll=2)
         if k == 0:
-            pl.semaphore_wait(barrier, DEVICES - 1)
+            pl.semaphore_wait(barrier, 10)
+            for sem, devices in ((core_sem, other_core), (y_sem, along_y), (z_sem, along_z)):
+                greet(sem, devices)
+                pl.semaphore_wait(sem, len(devices))
         ship_in(k, 0, 1)
         loop(1, GROUPS, lambda step: ship_in(k, step, 0))
         own_in[k].start()
+    for copy in late:
+        copy.wait()
     for k in range(CHUNKS):
         all_in(k).wait_recv()
         own_in[k].wait()
         convolve(k)
+        if k + 1 < CHUNKS:
+            all_in(k + 1).wait_send()
         ship_out(k, 0, 1)
         loop(1, GROUPS, lambda step: ship_out(k, step, 0))
         own_out[k].start()
-    gout_load.wait()
     stores = []
     for k in range(CHUNKS):
         all_out(k).wait_recv()
@@ -216,7 +258,8 @@
         stores.append(pltpu.make_async_copy(outv.at[:, lanes], out_hbm.at[:, lanes], store_sem.at[k]))
         stores[k].start()
     for k in range(CHUNKS):
-        all_in(k).wait_send()
+        if k == 0:
+            all_in(k).wait_send()
         all_out(k).wait_send()
         stores[k].wait()
 
@@ -224,26 +267,29 @@
 def shards(gate_in, value_in, gate_out, filters, skip_bias):
     rows, channels = gate_in.shape
     any_spec = pl.BlockSpec(memory_space=pl.ANY)
-    vmem_spec = pl.BlockSpec(memory_space=pltpu.VMEM)
     full = pltpu.VMEM((rows, channels), BF)
-    dma = pltpu.SemaphoreType.DMA
+    dma, regular = pltpu.SemaphoreType.DMA, pltpu.SemaphoreType.REGULAR
     return pl.pallas_call(
         kernel,
         out_shape=jax.ShapeDtypeStruct((rows, channels), BF),
-        in_specs=[any_spec] * 4 + [vmem_spec] * 7,
+        in_specs=[any_spec] * 7,
         out_specs=any_spec,
         scratch_shapes=[
-            full, full, full, full, full,
+            full, full, full, full,
+            pltpu.VMEM((1, channels), F32), pltpu.VMEM((896, 256), BF), pltpu.VMEM((2, 128, 128), F32),
+            full,
             pltpu.VMEM((CHUNKS, GROUPS, MEMBERS, 2, SHARE, BLOCK), BF),
             pltpu.VMEM((CHUNKS, DEVICES, 2, SHARE, BLOCK), BF),
             pltpu.VMEM((DEVICES * 2 * SHARE, BLOCK), F32),
             pltpu.VMEM((DEVICES * SHARE, BLOCK), F32),
+            pltpu.VMEM((512, 256), BF), pltpu.VMEM((256, 256), BF), pltpu.VMEM((256, 256), BF),
             pltpu.VMEM((CHUNKS, DEVICES, SHARE, BLOCK), BF),
             pltpu.VMEM((CHUNKS, GROUPS, MEMBERS, SHARE, BLOCK), BF),
-            dma((CHUNKS, 4)), dma((CHUNKS,)), dma((2, CHUNKS)),
+            dma((CHUNKS, 3)), dma((4,)), dma((CHUNKS,)), dma((2, CHUNKS)),
             dma((CHUNKS,)), dma((CHUNKS,)), dma((CHUNKS,)), dma((CHUNKS,)),
+            regular, regular, regular,
         ],
-        compiler_params=pltpu.CompilerParams(collective_id=0, has_side_effects=True, vmem_limit_bytes=40 * 2**20),
+        compiler_params=pltpu.CompilerParams(collective_id=0, has_side_effects=True, vmem_limit_bytes=63 * 2**20),
         name="gated_convolution",
     )(gate_in, value_in, gate_out, filters, skip_bias.reshape(1, channels), *tables())
 

time: 71.2 us -> 58.7 us (0.82)
  local copies, waits for them, and re-layouts: 11.7 us -> 2.29 us
  Pallas kernels: 58.2 us -> 55.7 us
    unnamed x23 -> x1, local copies, waits for them, and re-layouts: 11.7 us -> 2.29 us
    pallas_call x1, Pallas kernels: 58.2 us -> 55.7 us  [shards(): pl.pallas_call(kernel, out_shape=jax.ShapeDtypeStruct((rows, channels), B...]
where the time goes in v2:
time: 58.7 us; the launch traced here: 58 us
  Pallas kernels  55.7 us (95%)
  local copies, waits for them, and re-layouts  2.29 us (4%)
    pallas_call x1, Pallas kernels, shards(): pl.pallas_call(kernel, out_shape=jax.ShapeDtypeStruct((rows, channels), B...  55.7 us
    unnamed x1, local copies, waits for them, and re-layouts  2.29 us

profile of v2, /device:TPU:0, one launch (start us, length us, event | category | flops | bytes accessed | tf_op | source)
XLA Modules:
  0.0 58.0 jit_solution(15604455619815867402)
XLA Ops:
  0.0 55.7 %gated_convolution.1 = bf16[128,4096]{1,0:T(8,128)(2,1)} custom-call(bf16[128,4096]{1,0:T(8,128)(2,1)} %gate_hbm.1, bf16[128,4096]{1,0:T(8,128)(2,1)} %value_hbm.1, bf16[128,4096]{1,0:T(8,128)(2,1)} %gout_hbm.1, bf16[128,4096]{1,0:T(8,128)(2,1)} %filt_hbm.1, f32[1,4096]{1,0:T(1,128)} %bitcast.1, bf16[896,256]{1,0:T(8,128)(2,1)} %constant.4.clone.square_hbm, ...), custom_call_target="tpu_custom_call" | custom-call | tf_op jit(solution)/shard_map/gated_convolution/pallas_call | solution.py:272
  55.7 2.3 %copy.9 = bf16[128,4096]{1,0:T(8,128)(2,1)} copy(bf16[128,4096]{1,0:T(8,128)(2,1)} %gated_convolution.1) | data formatting | bytes 2097152
